TPU v7x, 512 devices: a whole 4x8x8 slice. The times are simulated.
512 devices in a mesh: lon: 64 (over z_lo, y, core), plane: 8 (over z_hi, x).
Axes of the slice: x: 4, y: 8, z: 8 (z_hi: 2, z_lo: 4; z = z_hi * 4 + z_lo), core: 2. Of those that a mesh axis runs over, the one named last changes fastest.
Arguments:
- potential: float32 [8, 256, 16384], P('plane', None, 'lon'), may hold values from -0.6 to 0.6
- lens_weight: float32 [8, 8], P('plane'), may hold values from 0.1 to 0.3
- cycle_shift: int32 [2, 256], replicated, may hold values from -3 to 2
- cycle_weight: int32 [2, 256], replicated, may hold values from 0 to 16
- cycle_scale: float32 [256], replicated, may hold values from 1 to 2
Outputs:
- displacement: float32 [8, 2, 256, 16384], P('plane', None, None, 'lon')
- jacobian: float32 [8, 4, 256, 16384], P('plane', None, None, 'lon')
All inputs are finite; a program needn't handle non-finite values.
Results may differ from a plain program's by a relative error of at most 0.00002.
Values sent between devices are 32-bit elements; how exact they have to be, the bound alone decides.
No kernel may reach another device: no remote copies, remote signals or barrier semaphores. Data moves between devices by JAX's collectives and lax.ppermute only.
A program may use at most 64 MiB of HBM per device.

v0:
```python
import jax
import jax.numpy as jnp
from jax import lax
from jax.sharding import PartitionSpec as P

HALO = 4


def shifted(value, axis, steps):
    count = lax.axis_size(axis)
    pairs = [(source, (source + steps) % count) for source in range(count)]
    return lax.ppermute(value, axis, pairs)


def extended(block, sides, width):
    for axis, dim in sides:
        count = lax.axis_size(axis)
        forward = [(i, i + 1) for i in range(count - 1)]
        forward.append((count - 1, 0))
        backward = [(target, source) for source, target in forward]
        low = lax.ppermute(
            lax.slice_in_dim(block, block.shape[dim] - width, None, axis=dim), axis, forward
        )
        high = lax.ppermute(lax.slice_in_dim(block, 0, width, axis=dim), axis, backward)
        block = jnp.concatenate([low, block, high], axis=dim)
    return block


def from_root(shard, axis, root):
    mine = lax.axis_index(axis) == root
    return lax.psum(jnp.where(mine, shard, jnp.zeros_like(shard)), axis)


def pick_cycle(row_block, shifts, offset, width):
    result = jnp.zeros((row_block.shape[0], width), jnp.float32)
    for delta in range(-3, 3):
        start = HALO + delta + offset
        result = jnp.where(shifts[:, None] == delta, row_block[:, start : start + width], result)
    return result


def cycle_value(row_block, shifts, weights, offset, width):
    frac = weights.astype(jnp.float32)[:, None] / 16.0
    first = pick_cycle(row_block, shifts, offset, width)
    second = pick_cycle(row_block, shifts, offset + 1, width)
    return (1.0 - frac) * first + frac * second


def derivatives(padded, cycle_shift, cycle_weight, cycle_scale):
    width = padded.shape[1] - 2 * HALO
    north_rows = padded[:-2]
    south_rows = padded[2:]
    middle = padded[1:-1]
    north = [
        cycle_value(north_rows, cycle_shift[0], cycle_weight[0], offset, width)
        for offset in (-1, 0, 1)
    ]
    south = [
        cycle_value(south_rows, cycle_shift[1], cycle_weight[1], offset, width)
        for offset in (-1, 0, 1)
    ]
    center = [middle[:, HALO + offset : HALO + offset + width] for offset in (-1, 0, 1)]
    metric = cycle_scale[:, None]
    alpha_t = 0.5 * (south[1] - north[1])
    alpha_p = 0.5 * metric * (center[2] - center[0])
    shear_tt = south[1] - 2.0 * center[1] + north[1]
    shear_pp = metric * metric * (center[2] - 2.0 * center[1] + center[0])
    shear_tp = 0.25 * metric * (south[2] - south[0] - north[2] + north[0])
    return (alpha_t, alpha_p, shear_tt, shear_pp, shear_tp)


def advance(state, fields, gain):
    disp_t, disp_p, a_zz, a_zo, a_oz, a_oo = state
    alpha_t, alpha_p, shear_tt, shear_pp, shear_tp = fields
    new_t = disp_t - gain * (alpha_t + shear_tt * disp_t + shear_tp * disp_p)
    new_p = disp_p - gain * (alpha_p + shear_tp * disp_t + shear_pp * disp_p)
    b_zz = a_zz - gain * (shear_tt * a_zz + shear_tp * a_oz)
    b_zo = a_zo - gain * (shear_tt * a_zo + shear_tp * a_oo)
    b_oz = a_oz - gain * (shear_tp * a_zz + shear_pp * a_oz)
    b_oo = a_oo - gain * (shear_tp * a_zo + shear_pp * a_oo)
    return (new_t, new_p, b_zz, b_zo, b_oz, b_oo)


def pad_rows(tile):
    return jnp.pad(tile, ((1, 1), (0, 0)))


def per_device(potential, lens_weight, cycle_shift, cycle_weight, cycle_scale):
    planes = lax.axis_size("plane")
    lon_count = lax.axis_size("lon")
    by_tiles = lon_count - lon_count // 4
    rows_count = potential.shape[1]
    width = potential.shape[2]
    gains = lens_weight[0]
    zeros = jnp.zeros((rows_count, width), jnp.float32)
    ones = jnp.ones((rows_count, width), jnp.float32)
    state = (zeros, zeros, ones, zeros, zeros, ones)
    for plane_k in range(planes):
        turned = shifted(from_root(potential, "plane", plane_k), "lon", by_tiles)
        sky_tile = extended(turned, (("lon", 2),), HALO)[0]
        fields = derivatives(pad_rows(sky_tile), cycle_shift, cycle_weight, cycle_scale)
        state = advance(state, fields, gains[plane_k])
    displacement = jnp.stack(state[0:2])[None]
    jacobian = jnp.stack(state[2:6])[None]
    return (displacement, jacobian)


def solution(mesh):
    in_specs = (P("plane", None, "lon"), P("plane", None), P(), P(), P())
    out_specs = (P("plane", None, None, "lon"), P("plane", None, None, "lon"))
    return jax.shard_map(
        per_device, mesh=mesh, in_specs=in_specs, out_specs=out_specs, check_vma=False
    )
```

profile of v0, /device:TPU:6, one launch (start us, length us, event | category | flops | bytes accessed | tf_op | source)
XLA Modules:
  0.0 324.3 jit_solution(139829288068550160)
XLA Ops:
  7.2 2.3 broadcast_select_fusion
  10.9 149.9 %all-reduce.11.cloned.1.call-done = (f32[1,256,256]{2,1,0:T(8,128)}, f32[1,256,256]{2,1,0:T(8,128)}, f32[1,256,256]{2,1,0:T(8,128)}, f32[1,256,256]{2,1,0:T(8,12...) async-done(((f32[1,256,256]{2,1,0:T(8,128)}, f32[1,256,256]{2,1,0:T(8,128)}, f32[1,256,256]{2,1,0:T(8,128)}, ...) | async-done | bytes 2097168 | tf_op jit(solution)/shard_map/psum | solution.py:31
  168.0 6.8 %collective-permute-start.9 = (f32[1,256,256]{2,1,0:T(8,128)}, f32[1,256,256]{2,1,0:T(8,128)S(1)}, u32[]{:S(2)}, u32[]{:S(2)}) collective-permute-start(f32[1,256,256]{2,1,0:T(8,128)} %get-tuple-element.17), channel_id=1, source_target_pairs={{0,384},{8,392},{16,400},{24,408},{32,416},{40,424},{48,432},{56,4... | collective-permute-start | bytes 786440 | tf_op jit(solution)/shard_map/ppermute | solution.py:12
  176.8 2.1 collective-permute-start.15
  179.0 2.5 collective-permute-start.18
  183.3 4.7 %collective-permute-start.21 = (f32[1,256,256]{2,1,0:T(8,128)S(1)}, f32[1,256,256]{2,1,0:T(8,128)S(1)}, u32[]{:S(2)}, u32[]{:S(2)}) collective-permute-start(f32[1,256,256]{2,1,0:T(8,128)S(1)} %copy-done.4), channel_id=1, source_target_pairs={{0,384},{8,392},{16,400},{24,408},{32,416},{40,424},{48,432},{56,4... | collective-permute-start | bytes 786440 | tf_op jit(solution)/shard_map/ppermute | solution.py:12
  190.9 3.6 %collective-permute-done.12 = f32[1,256,256]{2,1,0:T(8,128)S(1)} collective-permute-done((f32[1,256,256]{2,1,0:T(8,128)}, f32[1,256,256]{2,1,0:T(8,128)S(1)}, u32[]{:S(2)}, u32[]{:S(2)}) %collective-permute-start.12) | collective-permute-done | bytes 262176 | tf_op jit(solution)/shard_map/ppermute | solution.py:12
  194.5 4.0 %collective-permute-start.2 = (f32[1,256,4]{2,1,0:T(8,128)S(1)}, f32[1,256,4]{2,1,0:T(8,128)S(1)}, u32[]{:S(2)}, u32[]{:S(2)}) collective-permute-start(f32[1,256,4]{2,1,0:T(8,128)S(1)} %get-tuple-element.114), channel_id=1, source_target_pairs={{8,0},{16,8},{24,16},{32,24},{40,32},{48,40},{56,48},{64,56},{72,6... | collective-permute-start | bytes 12296 | tf_op jit(solution)/shard_map/ppermute | solution.py:24
  198.6 3.0 collective-permute-done.15
  203.5 4.5 %collective-permute-done.18 = f32[1,256,256]{2,1,0:T(8,128)S(1)} collective-permute-done((f32[1,256,256]{2,1,0:T(8,128)S(1)}, f32[1,256,256]{2,1,0:T(8,128)S(1)}, u32[]{:S(2)}, u32[]{:S(2)}) %collective-permute-start.18) | collective-permute-done | bytes 262176 | tf_op jit(solution)/shard_map/ppermute | solution.py:12
  208.0 3.1 collective-permute-start.5
  214.2 7.5 %collective-permute-start.8 = (f32[1,256,4]{2,1,0:T(8,128)S(1)}, f32[1,256,4]{2,1,0:T(8,128)S(1)}, u32[]{:S(2)}, u32[]{:S(2)}) collective-permute-start(f32[1,256,4]{2,1,0:T(8,128)S(1)} %get-tuple-element.112), channel_id=1, source_target_pairs={{8,0},{16,8},{24,16},{32,24},{40,32},{48,40},{56,48},{64,56},{72,6... | collective-permute-start | bytes 12296 | tf_op jit(solution)/shard_map/ppermute | solution.py:24
  221.8 1.9 collective-permute-start.10
  224.0 7.5 %collective-permute-start.11 = (f32[1,256,4]{2,1,0:T(8,128)S(1)}, f32[1,256,4]{2,1,0:T(8,128)S(1)}, u32[]{:S(2)}, u32[]{:S(2)}) collective-permute-start(f32[1,256,4]{2,1,0:T(8,128)S(1)} %get-tuple-element.118), channel_id=1, source_target_pairs={{8,0},{16,8},{24,16},{32,24},{40,32},{48,40},{56,48},{64,56},{72,6... | collective-permute-start | bytes 12296 | tf_op jit(solution)/shard_map/ppermute | solution.py:24
  231.5 1.9 collective-permute-start.13
  233.7 6.8 %multiply_subtract_fusion.25 = (f32[256,256]{1,0:T(8,128)S(1)}, f32[256,256]{1,0:T(8,128)S(1)}, f32[256,256]{1,0:T(8,128)S(1)}, f32[256,256]{1,0:T(8,128)S(1)}, ...) fusion(f32[]{:T(128)} %bitcast.4, f32[]{:T(128)} %bitcast, ...), kind=kLoop, calls=%fused_computation.47 | loop fusion | flops 13762560 | bytes 4206600 | tf_op jit(solution)/shard_map/sub | solution.py:77
  243.9 7.5 %collective-permute-start.14 = (f32[1,256,4]{2,1,0:T(8,128)S(1)}, f32[1,256,4]{2,1,0:T(8,128)S(1)}, u32[]{:S(2)}, u32[]{:S(2)}) collective-permute-start(f32[1,256,4]{2,1,0:T(8,128)S(1)} %get-tuple-element.110), channel_id=1, source_target_pairs={{8,0},{16,8},{24,16},{32,24},{40,32},{48,40},{56,48},{64,56},{72,6... | collective-permute-start | bytes 12296 | tf_op jit(solution)/shard_map/ppermute | solution.py:24
  253.6 7.5 %collective-permute-start.17 = (f32[1,256,4]{2,1,0:T(8,128)S(1)}, f32[1,256,4]{2,1,0:T(8,128)S(1)}, u32[]{:S(2)}, u32[]{:S(2)}) collective-permute-start(f32[1,256,4]{2,1,0:T(8,128)S(1)} %get-tuple-element.120), channel_id=1, source_target_pairs={{8,0},{16,8},{24,16},{32,24},{40,32},{48,40},{56,48},{64,56},{72,6... | collective-permute-start | bytes 12296 | tf_op jit(solution)/shard_map/ppermute | solution.py:24
  263.3 6.9 %multiply_subtract_fusion.21 = (f32[256,256]{1,0:T(8,128)S(1)}, f32[256,256]{1,0:T(8,128)S(1)}, f32[256,256]{1,0:T(8,128)S(1)}, f32[256,256]{1,0:T(8,128)S(1)}, ...) fusion(f32[]{:T(128)} %bitcast.8, ...), kind=kLoop, calls=%fused_computation.43 | loop fusion | flops 13893632 | bytes 4993032 | tf_op jit(solution)/shard_map/sub | solution.py:77
  274.5 7.5 %collective-permute-start.20 = (f32[1,256,4]{2,1,0:T(8,128)S(1)}, f32[1,256,4]{2,1,0:T(8,128)S(1)}, u32[]{:S(2)}, u32[]{:S(2)}) collective-permute-start(f32[1,256,4]{2,1,0:T(8,128)S(1)} %get-tuple-element.108), channel_id=1, source_target_pairs={{8,0},{16,8},{24,16},{32,24},{40,32},{48,40},{56,48},{64,56},{72,6... | collective-permute-start | bytes 12296 | tf_op jit(solution)/shard_map/ppermute | solution.py:24
  282.1 1.9 collective-permute-start.22
  284.3 7.7 %collective-permute-start.23 = (f32[1,256,4]{2,1,0:T(8,128)S(1)}, f32[1,256,4]{2,1,0:T(8,128)S(1)}, u32[]{:S(2)}, u32[]{:S(2)}) collective-permute-start(f32[1,256,4]{2,1,0:T(8,128)S(1)} %get-tuple-element.122), channel_id=1, source_target_pairs={{8,0},{16,8},{24,16},{32,24},{40,32},{48,40},{56,48},{64,56},{72,6... | collective-permute-start | bytes 12296 | tf_op jit(solution)/shard_map/ppermute | solution.py:24
  292.2 6.9 %multiply_subtract_fusion.17 = (f32[256,256]{1,0:T(8,128)S(1)}, f32[256,256]{1,0:T(8,128)S(1)}, f32[256,256]{1,0:T(8,128)S(1)}, f32[256,256]{1,0:T(8,128)S(1)}, ...) fusion(f32[]{:T(128)} %bitcast.12, ...), kind=kLoop, calls=%fused_computation.39 | loop fusion | flops 13893632 | bytes 4993032 | tf_op jit(solution)/shard_map/sub | solution.py:77
  304.0 7.0 %subtract_bitcast_fusion.3 = (f32[1,256,256]{2,1,0:T(8,128)S(1)}, f32[256,256]{1,0:T(8,128)S(1)}, f32[256,256]{1,0:T(8,128)S(1)}, f32[256,256]{1,0:T(8,128)S(1)}...) fusion(f32[]{:T(128)} %bitcast.16, ...), kind=kLoop, calls=%fused_computation.35 | loop fusion | flops 13893632 | bytes 4993032 | tf_op jit(solution)/shard_map/stack | solution.py:104
  (78 shorter events, 44.6 us)
Async XLA Ops:
  7.2 153.6 %all-reduce.11.cloned.1.call-start = ((), (), s32[]{:S(2)}) async-start(), calls=%async_computation | async-start | bytes 4194304 | tf_op jit(solution)/shard_map/psum | solution.py:31
  160.8 16.0 %collective-permute-start = (f32[1,256,256]{2,1,0:T(8,128)}, f32[1,256,256]{2,1,0:T(8,128)S(1)}, u32[]{:S(2)}, u32[]{:S(2)}) collective-permute-start(f32[1,256,256]{2,1,0:T(8,128)} %get-tuple-element.14), channel_id=1, source_target_pairs={{0,384},{8,392},{16,400},{24,408},{32,416},{40,424},{48,432},{56,4... | collective-permute-start | bytes 786440 | tf_op jit(solution)/shard_map/ppermute | solution.py:12
  166.1 17.2 %collective-permute-start.6 = (f32[1,256,256]{2,1,0:T(8,128)}, f32[1,256,256]{2,1,0:T(8,128)S(1)}, u32[]{:S(2)}, u32[]{:S(2)}) collective-permute-start(f32[1,256,256]{2,1,0:T(8,128)} %get-tuple-element.16), channel_id=1, source_target_pairs={{0,384},{8,392},{16,400},{24,408},{32,416},{40,424},{48,432},{56,4... | collective-permute-start | bytes 786440 | tf_op jit(solution)/shard_map/ppermute | solution.py:12
  168.0 20.9 %collective-permute-start.9 = (f32[1,256,256]{2,1,0:T(8,128)}, f32[1,256,256]{2,1,0:T(8,128)S(1)}, u32[]{:S(2)}, u32[]{:S(2)}) collective-permute-start(f32[1,256,256]{2,1,0:T(8,128)} %get-tuple-element.17), channel_id=1, source_target_pairs={{0,384},{8,392},{16,400},{24,408},{32,416},{40,424},{48,432},{56,4... | collective-permute-start | bytes 786440 | tf_op jit(solution)/shard_map/ppermute | solution.py:12
  174.8 19.7 %collective-permute-start.12 = (f32[1,256,256]{2,1,0:T(8,128)}, f32[1,256,256]{2,1,0:T(8,128)S(1)}, u32[]{:S(2)}, u32[]{:S(2)}) collective-permute-start(f32[1,256,256]{2,1,0:T(8,128)} %get-tuple-element.18), channel_id=1, source_target_pairs={{0,384},{8,392},{16,400},{24,408},{32,416},{40,424},{48,432},{56,4... | collective-permute-start | bytes 786440 | tf_op jit(solution)/shard_map/ppermute | solution.py:12
  176.8 24.7 %collective-permute-start.15 = (f32[1,256,256]{2,1,0:T(8,128)}, f32[1,256,256]{2,1,0:T(8,128)S(1)}, u32[]{:S(2)}, u32[]{:S(2)}) collective-permute-start(f32[1,256,256]{2,1,0:T(8,128)} %get-tuple-element.19), channel_id=1, source_target_pairs={{0,384},{8,392},{16,400},{24,408},{32,416},{40,424},{48,432},{56,4... | collective-permute-start | bytes 786440 | tf_op jit(solution)/shard_map/ppermute | solution.py:12
  179.0 29.0 %collective-permute-start.18 = (f32[1,256,256]{2,1,0:T(8,128)S(1)}, f32[1,256,256]{2,1,0:T(8,128)S(1)}, u32[]{:S(2)}, u32[]{:S(2)}) collective-permute-start(f32[1,256,256]{2,1,0:T(8,128)S(1)} %copy-done.5), channel_id=1, source_target_pairs={{0,384},{8,392},{16,400},{24,408},{32,416},{40,424},{48,432},{56,4... | collective-permute-start | bytes 786440 | tf_op jit(solution)/shard_map/ppermute | solution.py:12
  183.3 28.9 %collective-permute-start.21 = (f32[1,256,256]{2,1,0:T(8,128)S(1)}, f32[1,256,256]{2,1,0:T(8,128)S(1)}, u32[]{:S(2)}, u32[]{:S(2)}) collective-permute-start(f32[1,256,256]{2,1,0:T(8,128)S(1)} %copy-done.4), channel_id=1, source_target_pairs={{0,384},{8,392},{16,400},{24,408},{32,416},{40,424},{48,432},{56,4... | collective-permute-start | bytes 786440 | tf_op jit(solution)/shard_map/ppermute | solution.py:12
  188.9 25.3 %collective-permute-start.1 = (f32[1,256,4]{2,1,0:T(8,128)S(1)}, f32[1,256,4]{2,1,0:T(8,128)S(1)}, u32[]{:S(2)}, u32[]{:S(2)}) collective-permute-start(f32[1,256,4]{2,1,0:T(8,128)S(1)} %get-tuple-element.113), channel_id=1, source_target_pairs={{0,8},{8,16},{16,24},{24,32},{32,40},{40,48},{48,56},{56,64},{64,7... | collective-permute-start | bytes 12296 | tf_op jit(solution)/shard_map/ppermute | solution.py:21
  194.5 27.3 %collective-permute-start.2 = (f32[1,256,4]{2,1,0:T(8,128)S(1)}, f32[1,256,4]{2,1,0:T(8,128)S(1)}, u32[]{:S(2)}, u32[]{:S(2)}) collective-permute-start(f32[1,256,4]{2,1,0:T(8,128)S(1)} %get-tuple-element.114), channel_id=1, source_target_pairs={{8,0},{16,8},{24,16},{32,24},{40,32},{48,40},{56,48},{64,56},{72,6... | collective-permute-start | bytes 12296 | tf_op jit(solution)/shard_map/ppermute | solution.py:24
  201.5 22.4 %collective-permute-start.4 = (f32[1,256,4]{2,1,0:T(8,128)S(1)}, f32[1,256,4]{2,1,0:T(8,128)S(1)}, u32[]{:S(2)}, u32[]{:S(2)}) collective-permute-start(f32[1,256,4]{2,1,0:T(8,128)S(1)} %get-tuple-element.115), channel_id=1, source_target_pairs={{0,8},{8,16},{16,24},{24,32},{32,40},{40,48},{48,56},{56,64},{64,7... | collective-permute-start | bytes 12296 | tf_op jit(solution)/shard_map/ppermute | solution.py:21
  208.0 23.5 %collective-permute-start.5 = (f32[1,256,4]{2,1,0:T(8,128)S(1)}, f32[1,256,4]{2,1,0:T(8,128)S(1)}, u32[]{:S(2)}, u32[]{:S(2)}) collective-permute-start(f32[1,256,4]{2,1,0:T(8,128)S(1)} %get-tuple-element.116), channel_id=1, source_target_pairs={{8,0},{16,8},{24,16},{32,24},{40,32},{48,40},{56,48},{64,56},{72,6... | collective-permute-start | bytes 12296 | tf_op jit(solution)/shard_map/ppermute | solution.py:24
  212.2 31.7 %collective-permute-start.7 = (f32[1,256,4]{2,1,0:T(8,128)S(1)}, f32[1,256,4]{2,1,0:T(8,128)S(1)}, u32[]{:S(2)}, u32[]{:S(2)}) collective-permute-start(f32[1,256,4]{2,1,0:T(8,128)S(1)} %get-tuple-element.111), channel_id=1, source_target_pairs={{0,8},{8,16},{16,24},{24,32},{32,40},{40,48},{48,56},{56,64},{64,7... | collective-permute-start | bytes 12296 | tf_op jit(solution)/shard_map/ppermute | solution.py:21
  214.2 37.2 %collective-permute-start.8 = (f32[1,256,4]{2,1,0:T(8,128)S(1)}, f32[1,256,4]{2,1,0:T(8,128)S(1)}, u32[]{:S(2)}, u32[]{:S(2)}) collective-permute-start(f32[1,256,4]{2,1,0:T(8,128)S(1)} %get-tuple-element.112), channel_id=1, source_target_pairs={{8,0},{16,8},{24,16},{32,24},{40,32},{48,40},{56,48},{64,56},{72,6... | collective-permute-start | bytes 12296 | tf_op jit(solution)/shard_map/ppermute | solution.py:24
  221.8 31.8 %collective-permute-start.10 = (f32[1,256,4]{2,1,0:T(8,128)S(1)}, f32[1,256,4]{2,1,0:T(8,128)S(1)}, u32[]{:S(2)}, u32[]{:S(2)}) collective-permute-start(f32[1,256,4]{2,1,0:T(8,128)S(1)} %get-tuple-element.117), channel_id=1, source_target_pairs={{0,8},{8,16},{16,24},{24,32},{32,40},{40,48},{48,56},{56,64},{64,7... | collective-permute-start | bytes 12296 | tf_op jit(solution)/shard_map/ppermute | solution.py:21
  224.0 37.2 %collective-permute-start.11 = (f32[1,256,4]{2,1,0:T(8,128)S(1)}, f32[1,256,4]{2,1,0:T(8,128)S(1)}, u32[]{:S(2)}, u32[]{:S(2)}) collective-permute-start(f32[1,256,4]{2,1,0:T(8,128)S(1)} %get-tuple-element.118), channel_id=1, source_target_pairs={{8,0},{16,8},{24,16},{32,24},{40,32},{48,40},{56,48},{64,56},{72,6... | collective-permute-start | bytes 12296 | tf_op jit(solution)/shard_map/ppermute | solution.py:24
  231.5 43.0 %collective-permute-start.13 = (f32[1,256,4]{2,1,0:T(8,128)S(1)}, f32[1,256,4]{2,1,0:T(8,128)S(1)}, u32[]{:S(2)}, u32[]{:S(2)}) collective-permute-start(f32[1,256,4]{2,1,0:T(8,128)S(1)} %get-tuple-element.109), channel_id=1, source_target_pairs={{0,8},{8,16},{16,24},{24,32},{32,40},{40,48},{48,56},{56,64},{64,7... | collective-permute-start | bytes 12296 | tf_op jit(solution)/shard_map/ppermute | solution.py:21
  243.9 38.2 %collective-permute-start.14 = (f32[1,256,4]{2,1,0:T(8,128)S(1)}, f32[1,256,4]{2,1,0:T(8,128)S(1)}, u32[]{:S(2)}, u32[]{:S(2)}) collective-permute-start(f32[1,256,4]{2,1,0:T(8,128)S(1)} %get-tuple-element.110), channel_id=1, source_target_pairs={{8,0},{16,8},{24,16},{32,24},{40,32},{48,40},{56,48},{64,56},{72,6... | collective-permute-start | bytes 12296 | tf_op jit(solution)/shard_map/ppermute | solution.py:24
  251.4 32.8 %collective-permute-start.16 = (f32[1,256,4]{2,1,0:T(8,128)S(1)}, f32[1,256,4]{2,1,0:T(8,128)S(1)}, u32[]{:S(2)}, u32[]{:S(2)}) collective-permute-start(f32[1,256,4]{2,1,0:T(8,128)S(1)} %get-tuple-element.119), channel_id=1, source_target_pairs={{0,8},{8,16},{16,24},{24,32},{32,40},{40,48},{48,56},{56,64},{64,7... | collective-permute-start | bytes 12296 | tf_op jit(solution)/shard_map/ppermute | solution.py:21
  253.6 38.4 %collective-permute-start.17 = (f32[1,256,4]{2,1,0:T(8,128)S(1)}, f32[1,256,4]{2,1,0:T(8,128)S(1)}, u32[]{:S(2)}, u32[]{:S(2)}) collective-permute-start(f32[1,256,4]{2,1,0:T(8,128)S(1)} %get-tuple-element.120), channel_id=1, source_target_pairs={{8,0},{16,8},{24,16},{32,24},{40,32},{48,40},{56,48},{64,56},{72,6... | collective-permute-start | bytes 12296 | tf_op jit(solution)/shard_map/ppermute | solution.py:24
  261.2 42.4 %collective-permute-start.19 = (f32[1,256,4]{2,1,0:T(8,128)S(1)}, f32[1,256,4]{2,1,0:T(8,128)S(1)}, u32[]{:S(2)}, u32[]{:S(2)}) collective-permute-start(f32[1,256,4]{2,1,0:T(8,128)S(1)} %get-tuple-element.107), channel_id=1, source_target_pairs={{0,8},{8,16},{16,24},{24,32},{32,40},{40,48},{48,56},{56,64},{64,7... | collective-permute-start | bytes 12296 | tf_op jit(solution)/shard_map/ppermute | solution.py:21
  274.5 29.0 %collective-permute-start.20 = (f32[1,256,4]{2,1,0:T(8,128)S(1)}, f32[1,256,4]{2,1,0:T(8,128)S(1)}, u32[]{:S(2)}, u32[]{:S(2)}) collective-permute-start(f32[1,256,4]{2,1,0:T(8,128)S(1)} %get-tuple-element.108), channel_id=1, source_target_pairs={{8,0},{16,8},{24,16},{32,24},{40,32},{48,40},{56,48},{64,56},{72,6... | collective-permute-start | bytes 12296 | tf_op jit(solution)/shard_map/ppermute | solution.py:24
  282.1 21.7 %collective-permute-start.22 = (f32[1,256,4]{2,1,0:T(8,128)S(1)}, f32[1,256,4]{2,1,0:T(8,128)S(1)}, u32[]{:S(2)}, u32[]{:S(2)}) collective-permute-start(f32[1,256,4]{2,1,0:T(8,128)S(1)} %get-tuple-element.121), channel_id=1, source_target_pairs={{0,8},{8,16},{16,24},{24,32},{32,40},{40,48},{48,56},{56,64},{64,7... | collective-permute-start | bytes 12296 | tf_op jit(solution)/shard_map/ppermute | solution.py:21
  284.3 19.5 %collective-permute-start.23 = (f32[1,256,4]{2,1,0:T(8,128)S(1)}, f32[1,256,4]{2,1,0:T(8,128)S(1)}, u32[]{:S(2)}, u32[]{:S(2)}) collective-permute-start(f32[1,256,4]{2,1,0:T(8,128)S(1)} %get-tuple-element.122), channel_id=1, source_target_pairs={{8,0},{16,8},{24,16},{32,24},{40,32},{48,40},{56,48},{64,56},{72,6... | collective-permute-start | bytes 12296 | tf_op jit(solution)/shard_map/ppermute | solution.py:24
  (7 other events, 26.0 us)
Sparse Core Ops, SparseCore 0:
  12.1 148.6 all-reduce.10
where the time goes:
time: 325 us; the launch traced here: 324 us
  waiting for transfers between devices  165 us (51%)
  starting transfers between devices  91.6 us (28%)
  other arithmetic  50.1 us (15%)
  between operations  14.6 us (4%)
  local copies, waits for them, and re-layouts  3.43 us (1%)
    psum x1, waiting for transfers between devices, from_root(): return lax.psum(jnp.where(mine, shard, jnp.zeros_like(shard)), axis)  150 us
    ppermute x8, starting transfers between devices, extended(): lax.ppermute(lax.slice_in_dim(block, 0, width, axis=dim), axis, backward)  52.5 us
    ppermute x8, starting transfers between devices, shifted(): return lax.ppermute(value, axis, pairs)  23.7 us
    sub x3, other arithmetic, advance(): b_zz = a_zz - gain * (shear_tt * a_zz + shear_tp * a_oz)  20.6 us
    ppermute x8, starting transfers between devices, extended(): lax.ppermute(lax.slice_in_dim(block, block.shape[dim] - width, None, axis...  15.3 us
    ppermute x8, waiting for transfers between devices, shifted(): return lax.ppermute(value, axis, pairs)  14.6 us
    another operation x3, other arithmetic, per_device(): jacobian = jnp.stack(state[2:6])[None]  9.68 us
  transfers between devices with their start and end apart: 25, of which 7 were waited for; matrix products, arithmetic and copies ran while one was open for 11% of the time, Pallas kernels for 0%

commit v1 on v0

--- a/solution.py
+++ b/solution.py
@@ -4,6 +4,10 @@
 from jax.sharding import PartitionSpec as P
 
 HALO = 4
+
+
+def bring_leaf(chunk, dev_axis):
+    return jnp.sum(lax.all_gather(chunk, dev_axis), 0)
 
 
 def shifted(value, axis, steps):
@@ -28,7 +32,7 @@
 
 def from_root(shard, axis, root):
     mine = lax.axis_index(axis) == root
-    return lax.psum(jnp.where(mine, shard, jnp.zeros_like(shard)), axis)
+    return bring_leaf(jnp.where(mine, shard, jnp.zeros_like(shard)), axis)
 
 
 def pick_cycle(row_block, shifts, offset, width):

time: 325 us -> 809 us (2.49)
  waiting for transfers between devices: 165 us -> 628 us
  other arithmetic: 50.1 us -> 63.6 us
  starting transfers between devices: 91.6 us -> 99.8 us
    all_gather x0 -> x8, waiting for transfers between devices: none -> 624 us  [bring_leaf(): return jnp.sum(lax.all_gather(chunk, dev_axis), 0)]
    psum x1 -> x0, waiting for transfers between devices: 150 us -> none  [from_root(): return lax.psum(jnp.where(mine, shard, jnp.zeros_like(shard)), axis)]
    ppermute x8, waiting for transfers between devices: 14.6 us -> 0.02 us  [shifted(): return lax.ppermute(value, axis, pairs)]
    reduce_sum x0 -> x8, other arithmetic: none -> 14 us  [bring_leaf(): return jnp.sum(lax.all_gather(chunk, dev_axis), 0)]
  transfers between devices with their start and end apart: 25 -> 32, of which waited for: 7 -> 8; matrix products, arithmetic and copies ran while one was open for 11% -> 6% of each run, Pallas kernels for 0% -> 0%
where the time goes in v1:
time: 809 us; the launch traced here: 808 us
  waiting for transfers between devices  628 us (78%)
  starting transfers between devices  99.8 us (12%)
  other arithmetic  63.6 us (8%)
  between operations  14.8 us (2%)
    all_gather x8, waiting for transfers between devices, bring_leaf(): return jnp.sum(lax.all_gather(chunk, dev_axis), 0)  624 us
    ppermute x8, starting transfers between devices, extended(): lax.ppermute(lax.slice_in_dim(block, 0, width, axis=dim), axis, backward)  60.6 us
    ppermute x8, starting transfers between devices, shifted(): return lax.ppermute(value, axis, pairs)  23.6 us
    sub x3, other arithmetic, advance(): b_zz = a_zz - gain * (shear_tt * a_zz + shear_tp * a_oz)  20.5 us
  transfers between devices with their start and end apart: 32, of which 8 were waited for; matrix products, arithmetic and copies ran while one was open for 6% of the time, Pallas kernels for 0%

profile of v1, /device:TPU:6, one launch (start us, length us, event | category | flops | bytes accessed | tf_op | source)
XLA Modules:
  0.0 807.7 jit_solution(8113719325465175573)
XLA Ops:
  14.3 83.3 %all-gather.19.cloned.1.call-done = f32[8,256,256]{2,1,0:T(8,128)} async-done(((f32[1,256,256]{2,1,0:T(8,128)}), f32[8,256,256]{2,1,0:T(8,128)}) %all-gather.19.cloned.1.call-update) | async-done | bytes 2097168 | tf_op jit(solution)/shard_map/all_gather | solution.py:10
  99.4 2.9 collective-permute-start.3
  102.5 76.3 %all-gather.17.cloned.1.call-done = f32[8,256,256]{2,1,0:T(8,128)} async-done(((f32[1,256,256]{2,1,0:T(8,128)}), f32[8,256,256]{2,1,0:T(8,128)}) %all-gather.17.cloned.1.call-update) | async-done | bytes 2097168 | tf_op jit(solution)/shard_map/all_gather | solution.py:10
  180.5 2.9 collective-permute-start
  184.1 75.7 %all-gather.23.cloned.1.call-done = f32[8,256,256]{2,1,0:T(8,128)} async-done(((f32[1,256,256]{2,1,0:T(8,128)}), f32[8,256,256]{2,1,0:T(8,128)}) %all-gather.23.cloned.1.call-update) | async-done | bytes 2097168 | tf_op jit(solution)/shard_map/all_gather | solution.py:10
  264.5 76.2 %all-gather.21.cloned.1.call-done = f32[8,256,256]{2,1,0:T(8,128)} async-done(((f32[1,256,256]{2,1,0:T(8,128)}), f32[8,256,256]{2,1,0:T(8,128)}) %all-gather.21.cloned.1.call-update) | async-done | bytes 2097168 | tf_op jit(solution)/shard_map/all_gather | solution.py:10
  345.3 76.8 %all-gather.27.cloned.1.call-done = f32[8,256,256]{2,1,0:T(8,128)} async-done(((f32[1,256,256]{2,1,0:T(8,128)}), f32[8,256,256]{2,1,0:T(8,128)}) %all-gather.27.cloned.1.call-update) | async-done | bytes 2097168 | tf_op jit(solution)/shard_map/all_gather | solution.py:10
  426.8 76.2 %all-gather.25.cloned.1.call-done = f32[8,256,256]{2,1,0:T(8,128)} async-done(((f32[1,256,256]{2,1,0:T(8,128)}), f32[8,256,256]{2,1,0:T(8,128)}) %all-gather.25.cloned.1.call-update) | async-done | bytes 2097168 | tf_op jit(solution)/shard_map/all_gather | solution.py:10
  504.8 79.3 %all-gather.31.cloned.1.call-done = f32[8,256,256]{2,1,0:T(8,128)} async-done(((f32[1,256,256]{2,1,0:T(8,128)}), f32[8,256,256]{2,1,0:T(8,128)}) %all-gather.31.cloned.1.call-update) | async-done | bytes 2097168 | tf_op jit(solution)/shard_map/all_gather | solution.py:10
  585.8 79.9 %all-gather.29.cloned.1.call-done = f32[8,256,256]{2,1,0:T(8,128)} async-done(((f32[1,256,256]{2,1,0:T(8,128)}), f32[8,256,256]{2,1,0:T(8,128)}) %all-gather.29.cloned.1.call-update) | async-done | bytes 2097168 | tf_op jit(solution)/shard_map/all_gather | solution.py:10
  667.4 2.9 collective-permute-start.12
  673.2 3.4 collective-permute-start.18
  678.8 7.5 collective-permute-start.5
  688.5 7.5 collective-permute-start.2
  698.2 7.5 collective-permute-start.11
  707.9 7.5 collective-permute-start.8
  717.6 6.8 multiply_subtract_fusion.25
  727.8 7.5 collective-permute-start.17
  737.5 7.5 collective-permute-start.14
  747.2 6.8 multiply_subtract_fusion.21
  758.2 7.5 collective-permute-start.23
  767.9 7.7 collective-permute-start.20
  775.8 6.9 multiply_subtract_fusion.17
  787.6 6.9 subtract_bitcast_fusion.3
  (103 shorter events, 69.1 us)
Async XLA Ops:
  7.2 90.5 %all-gather.19.cloned.1.call-start = ((), (), s32[]{:S(2)}) async-start(), calls=%async_computation.1 | async-start | bytes 2359296 | tf_op jit(solution)/shard_map/all_gather | solution.py:10
  9.6 169.2 %all-gather.17.cloned.1.call-start = ((), (), s32[]{:S(2)}) async-start(), calls=%async_computation | async-start | bytes 2359296 | tf_op jit(solution)/shard_map/all_gather | solution.py:10
  10.3 249.5 %all-gather.23.cloned.1.call-start = ((), (), s32[]{:S(2)}) async-start(), calls=%async_computation.3 | async-start | bytes 2359296 | tf_op jit(solution)/shard_map/all_gather | solution.py:10
  11.0 329.6 %all-gather.21.cloned.1.call-start = ((), (), s32[]{:S(2)}) async-start(), calls=%async_computation.2 | async-start | bytes 2359296 | tf_op jit(solution)/shard_map/all_gather | solution.py:10
  11.6 410.5 %all-gather.27.cloned.1.call-start = ((), (), s32[]{:S(2)}) async-start(), calls=%async_computation.5 | async-start | bytes 2359296 | tf_op jit(solution)/shard_map/all_gather | solution.py:10
  12.2 490.8 %all-gather.25.cloned.1.call-start = ((), (), s32[]{:S(2)}) async-start(), calls=%async_computation.4 | async-start | bytes 2359296 | tf_op jit(solution)/shard_map/all_gather | solution.py:10
  12.8 571.3 %all-gather.31.cloned.1.call-start = ((), (), s32[]{:S(2)}) async-start(), calls=%async_computation.7 | async-start | bytes 2359296 | tf_op jit(solution)/shard_map/all_gather | solution.py:10
  13.5 652.1 %all-gather.29.cloned.1.call-start = ((), (), s32[]{:S(2)}) async-start(), calls=%async_computation.6 | async-start | bytes 2359296 | tf_op jit(solution)/shard_map/all_gather | solution.py:10
  99.4 568.0 %collective-permute-start.3 = (f32[1,256,256]{2,1,0:T(8,128)S(1)}, f32[1,256,256]{2,1,0:T(8,128)S(1)}, u32[]{:S(2)}, u32[]{:S(2)}) collective-permute-start(f32[1,256,256]{2,1,0:T(8,128)S(1)} %bitcast.50), channel_id=1, source_target_pairs={{0,384},{8,392},{16,400},{24,408},{32,416},{40,424},{48,432},{56,4... | collective-permute-start | bytes 786440 | tf_op jit(solution)/shard_map/ppermute | solution.py:16
  180.5 490.0 %collective-permute-start = (f32[1,256,256]{2,1,0:T(8,128)S(1)}, f32[1,256,256]{2,1,0:T(8,128)S(1)}, u32[]{:S(2)}, u32[]{:S(2)}) collective-permute-start(f32[1,256,256]{2,1,0:T(8,128)S(1)} %bitcast.53), channel_id=1, source_target_pairs={{0,384},{8,392},{16,400},{24,408},{32,416},{40,424},{48,432},{56,4... | collective-permute-start | bytes 786440 | tf_op jit(solution)/shard_map/ppermute | solution.py:16
  261.5 411.7 %collective-permute-start.9 = (f32[1,256,256]{2,1,0:T(8,128)S(1)}, f32[1,256,256]{2,1,0:T(8,128)S(1)}, u32[]{:S(2)}, u32[]{:S(2)}) collective-permute-start(f32[1,256,256]{2,1,0:T(8,128)S(1)} %bitcast.57), channel_id=1, source_target_pairs={{0,384},{8,392},{16,400},{24,408},{32,416},{40,424},{48,432},{56,4... | collective-permute-start | bytes 786440 | tf_op jit(solution)/shard_map/ppermute | solution.py:16
  342.4 334.3 %collective-permute-start.6 = (f32[1,256,256]{2,1,0:T(8,128)S(1)}, f32[1,256,256]{2,1,0:T(8,128)S(1)}, u32[]{:S(2)}, u32[]{:S(2)}) collective-permute-start(f32[1,256,256]{2,1,0:T(8,128)S(1)} %bitcast.56), channel_id=1, source_target_pairs={{0,384},{8,392},{16,400},{24,408},{32,416},{40,424},{48,432},{56,4... | collective-permute-start | bytes 786440 | tf_op jit(solution)/shard_map/ppermute | solution.py:16
  423.9 254.9 %collective-permute-start.15 = (f32[1,256,256]{2,1,0:T(8,128)S(1)}, f32[1,256,256]{2,1,0:T(8,128)S(1)}, u32[]{:S(2)}, u32[]{:S(2)}) collective-permute-start(f32[1,256,256]{2,1,0:T(8,128)S(1)} %bitcast.55), channel_id=1, source_target_pairs={{0,384},{8,392},{16,400},{24,408},{32,416},{40,424},{48,432},{56,4... | collective-permute-start | bytes 786440 | tf_op jit(solution)/shard_map/ppermute | solution.py:16
  688.5 27.0 %collective-permute-start.2 = (f32[1,256,4]{2,1,0:T(8,128)S(1)}, f32[1,256,4]{2,1,0:T(8,128)S(1)}, u32[]{:S(2)}, u32[]{:S(2)}) collective-permute-start(f32[1,256,4]{2,1,0:T(8,128)S(1)} %get-tuple-element.114), channel_id=1, source_target_pairs={{8,0},{16,8},{24,16},{32,24},{40,32},{48,40},{56,48},{64,56},{72,6... | collective-permute-start | bytes 12296 | tf_op jit(solution)/shard_map/ppermute | solution.py:28
  696.1 31.7 %collective-permute-start.10 = (f32[1,256,4]{2,1,0:T(8,128)S(1)}, f32[1,256,4]{2,1,0:T(8,128)S(1)}, u32[]{:S(2)}, u32[]{:S(2)}) collective-permute-start(f32[1,256,4]{2,1,0:T(8,128)S(1)} %get-tuple-element.117), channel_id=1, source_target_pairs={{0,8},{8,16},{16,24},{24,32},{32,40},{40,48},{48,56},{56,64},{64,7... | collective-permute-start | bytes 12296 | tf_op jit(solution)/shard_map/ppermute | solution.py:25
  698.2 37.2 %collective-permute-start.11 = (f32[1,256,4]{2,1,0:T(8,128)S(1)}, f32[1,256,4]{2,1,0:T(8,128)S(1)}, u32[]{:S(2)}, u32[]{:S(2)}) collective-permute-start(f32[1,256,4]{2,1,0:T(8,128)S(1)} %get-tuple-element.118), channel_id=1, source_target_pairs={{8,0},{16,8},{24,16},{32,24},{40,32},{48,40},{56,48},{64,56},{72,6... | collective-permute-start | bytes 12296 | tf_op jit(solution)/shard_map/ppermute | solution.py:28
  705.7 31.8 %collective-permute-start.7 = (f32[1,256,4]{2,1,0:T(8,128)S(1)}, f32[1,256,4]{2,1,0:T(8,128)S(1)}, u32[]{:S(2)}, u32[]{:S(2)}) collective-permute-start(f32[1,256,4]{2,1,0:T(8,128)S(1)} %get-tuple-element.111), channel_id=1, source_target_pairs={{0,8},{8,16},{16,24},{24,32},{32,40},{40,48},{48,56},{56,64},{64,7... | collective-permute-start | bytes 12296 | tf_op jit(solution)/shard_map/ppermute | solution.py:25
  707.9 37.2 %collective-permute-start.8 = (f32[1,256,4]{2,1,0:T(8,128)S(1)}, f32[1,256,4]{2,1,0:T(8,128)S(1)}, u32[]{:S(2)}, u32[]{:S(2)}) collective-permute-start(f32[1,256,4]{2,1,0:T(8,128)S(1)} %get-tuple-element.112), channel_id=1, source_target_pairs={{8,0},{16,8},{24,16},{32,24},{40,32},{48,40},{56,48},{64,56},{72,6... | collective-permute-start | bytes 12296 | tf_op jit(solution)/shard_map/ppermute | solution.py:28
  715.4 42.7 %collective-permute-start.16 = (f32[1,256,4]{2,1,0:T(8,128)S(1)}, f32[1,256,4]{2,1,0:T(8,128)S(1)}, u32[]{:S(2)}, u32[]{:S(2)}) collective-permute-start(f32[1,256,4]{2,1,0:T(8,128)S(1)} %get-tuple-element.119), channel_id=1, source_target_pairs={{0,8},{8,16},{16,24},{24,32},{32,40},{40,48},{48,56},{56,64},{64,7... | collective-permute-start | bytes 12296 | tf_op jit(solution)/shard_map/ppermute | solution.py:25
  727.8 37.9 %collective-permute-start.17 = (f32[1,256,4]{2,1,0:T(8,128)S(1)}, f32[1,256,4]{2,1,0:T(8,128)S(1)}, u32[]{:S(2)}, u32[]{:S(2)}) collective-permute-start(f32[1,256,4]{2,1,0:T(8,128)S(1)} %get-tuple-element.120), channel_id=1, source_target_pairs={{8,0},{16,8},{24,16},{32,24},{40,32},{48,40},{56,48},{64,56},{72,6... | collective-permute-start | bytes 12296 | tf_op jit(solution)/shard_map/ppermute | solution.py:28
  735.4 32.5 %collective-permute-start.13 = (f32[1,256,4]{2,1,0:T(8,128)S(1)}, f32[1,256,4]{2,1,0:T(8,128)S(1)}, u32[]{:S(2)}, u32[]{:S(2)}) collective-permute-start(f32[1,256,4]{2,1,0:T(8,128)S(1)} %get-tuple-element.109), channel_id=1, source_target_pairs={{0,8},{8,16},{16,24},{24,32},{32,40},{40,48},{48,56},{56,64},{64,7... | collective-permute-start | bytes 12296 | tf_op jit(solution)/shard_map/ppermute | solution.py:25
  737.5 38.1 %collective-permute-start.14 = (f32[1,256,4]{2,1,0:T(8,128)S(1)}, f32[1,256,4]{2,1,0:T(8,128)S(1)}, u32[]{:S(2)}, u32[]{:S(2)}) collective-permute-start(f32[1,256,4]{2,1,0:T(8,128)S(1)} %get-tuple-element.110), channel_id=1, source_target_pairs={{8,0},{16,8},{24,16},{32,24},{40,32},{48,40},{56,48},{64,56},{72,6... | collective-permute-start | bytes 12296 | tf_op jit(solution)/shard_map/ppermute | solution.py:28
  745.1 42.1 %collective-permute-start.22 = (f32[1,256,4]{2,1,0:T(8,128)S(1)}, f32[1,256,4]{2,1,0:T(8,128)S(1)}, u32[]{:S(2)}, u32[]{:S(2)}) collective-permute-start(f32[1,256,4]{2,1,0:T(8,128)S(1)} %get-tuple-element.121), channel_id=1, source_target_pairs={{0,8},{8,16},{16,24},{24,32},{32,40},{40,48},{48,56},{56,64},{64,7... | collective-permute-start | bytes 12296 | tf_op jit(solution)/shard_map/ppermute | solution.py:25
  758.2 29.0 %collective-permute-start.23 = (f32[1,256,4]{2,1,0:T(8,128)S(1)}, f32[1,256,4]{2,1,0:T(8,128)S(1)}, u32[]{:S(2)}, u32[]{:S(2)}) collective-permute-start(f32[1,256,4]{2,1,0:T(8,128)S(1)} %get-tuple-element.122), channel_id=1, source_target_pairs={{8,0},{16,8},{24,16},{32,24},{40,32},{48,40},{56,48},{64,56},{72,6... | collective-permute-start | bytes 12296 | tf_op jit(solution)/shard_map/ppermute | solution.py:28
  (12 other events, 446.8 us)
Sparse Core Ops, SparseCore 0:
  11.2 86.4 all-gather.18
  100.9 77.7 all-gather.16
  181.9 77.7 all-gather.22
  262.8 77.7 all-gather.20
  344.3 77.7 all-gather.26
  425.2 77.7 all-gather.24
  506.2 77.7 all-gather.30
  587.8 77.7 all-gather.28
